TPU v7x, 256 devices: a whole 4x4x8 slice. The times are simulated.
256 devices in a mesh: leaf: 32 (over x, y, core), front: 8 (over z).
Axes of the slice: x: 4, y: 4, z: 8, core: 2. Of those that a mesh axis runs over, the one named last changes fastest.
Arguments:
- child_updates: float32 [32768, 1024], P('leaf', 'front'), as said below
- initial_one: float32 [32768, 2048], P('leaf', 'front'), as said below
- initial_two: float32 [16384, 2048], P('leaf', 'front'), as said below
- pattern_one: int32 [16, 16, 16], replicated, may hold values 0 or 1
- pattern_two: int32 [8, 16, 16], replicated, may hold values 0 or 1
- parent_map_one: int32 [16, 2, 16], replicated, may hold values from 0 to 15, each once within a row
- parent_map_two: int32 [8, 2, 16], replicated, may hold values from 0 to 15, each once within a row
Outputs:
- factor_one: float32 [32768, 1024], P('leaf', 'front')
- factor_two: float32 [16384, 1024], P('leaf', 'front')
- schur_two: float32 [8192, 1024], P('leaf', 'front')
Inputs may be any that keep to these rules, and one draw needn't show every extreme that they name: `parent_map_one`: each row is a permutation of 0 to 15; only its first 8 entries are used. `parent_map_two`: each row is a permutation of 0 to 15; only its first 8 entries are used. `initial_one`: each 2048 x 2048 front block is symmetric, and positive definite after any symmetric block mask. `initial_two`: each 2048 x 2048 front block is symmetric, and positive definite after any symmetric block mask. `child_updates`: each 1024 x 1024 matrix is symmetric positive definite.
All inputs are finite; a program needn't handle non-finite values.
Results may differ from a plain program's by a relative error of at most 0.0003.
Values sent between devices are 32-bit elements; how exact they have to be, the bound alone decides.
No kernel may reach another device: no remote copies, remote signals or barrier semaphores. Data moves between devices by JAX's collectives and lax.ppermute only.
A program may use at most 128 MiB of HBM per device.

v0:
```python
import jax
import jax.numpy as jnp
from jax import lax
from jax.sharding import PartitionSpec as P

BLK = 128
SEP = 1024
UPD = 1024
FR = 2048
HIGHEST = lax.Precision.HIGHEST


def swapped(block, axis, stride):
    count = lax.axis_size(axis)
    route = []
    for low in range(count):
        high = low | 1 << stride
        if high != low and high < count:
            route += [(low, high), (high, low)]
    return lax.ppermute(block, axis, route)


def spread(block, axis, holder):
    block = jnp.where(lax.axis_index(axis) == holder, block, jnp.zeros_like(block))
    return lax.psum(block, axis)


def solve_rows(chol_block, right_side):
    return jax.scipy.linalg.solve_triangular(chol_block, right_side.T, lower=True).T


def gather_subcube(pieces, level_depth, leaf_index):
    for bit_number in range(level_depth):
        partner = swapped(pieces, "leaf", bit_number)
        upper_half = leaf_index >> bit_number & 1 == 1
        pieces = jnp.where(
            upper_half, jnp.concatenate([partner, pieces], 0), jnp.concatenate([pieces, partner], 0)
        )
    return pieces


def fetch_rows(pieces, wanted, level_depth, leaf_index):
    columns = pieces.shape[1]
    full_panel = gather_subcube(pieces, level_depth, leaf_index)
    return jnp.take(full_panel.reshape(FR // BLK, BLK, columns), wanted, axis=0).reshape(
        wanted.shape[0] * BLK, columns
    )


def merge_halves(placed, level_depth, leaf_index):
    for bit_number in reversed(range(level_depth)):
        middle = placed.shape[0] // 2
        upper_half = leaf_index >> bit_number & 1 == 1
        kept_half = jnp.where(upper_half, placed[middle:], placed[:middle])
        given_half = jnp.where(upper_half, placed[:middle], placed[middle:])
        placed = kept_half + swapped(given_half, "leaf", bit_number)
    return placed


def assemble(
    child_tile, initial, pattern, parent_map, level_depth, leaf_index, front_index, col_blocks
):
    group_share = 2**level_depth
    child_share = group_share // 2
    front_group = leaf_index // group_share
    child_side = leaf_index // child_share % 2
    child_sub = leaf_index % child_share
    sub_index = leaf_index % group_share
    update_blocks = UPD // BLK
    front_blocks = FR // BLK
    tile_cols = 2 * col_blocks * BLK
    gathered = lax.all_gather(child_tile, "front", axis=1, tiled=True)
    child_rows = gathered.shape[0]
    child_row_blocks = child_rows // BLK
    both_maps = lax.dynamic_index_in_dim(parent_map, front_group, 0, keepdims=False)
    block_map = lax.dynamic_index_in_dim(both_maps, child_side, 0, keepdims=False)[:update_blocks]
    target_cols = 2 * col_blocks * front_index + jnp.arange(2 * col_blocks, dtype=jnp.int32)
    col_pick = (block_map[:, None] == target_cols[None, :]).astype(jnp.float32)
    picked = jnp.einsum(
        "rik,it->rtk", gathered.reshape(child_rows, update_blocks, BLK), col_pick, precision=HIGHEST
    )
    my_map = lax.dynamic_slice_in_dim(block_map, child_sub * child_row_blocks, child_row_blocks)
    row_place = (jnp.arange(front_blocks, dtype=jnp.int32)[:, None] == my_map[None, :]).astype(
        jnp.float32
    )
    placed = jnp.einsum(
        "ba,akc->bkc",
        row_place,
        picked.reshape(child_row_blocks, BLK, tile_cols),
        precision=HIGHEST,
    ).reshape(FR, tile_cols)
    merged = merge_halves(placed, level_depth, leaf_index)
    own_blocks = front_blocks // group_share
    whole_pattern = lax.dynamic_index_in_dim(pattern, front_group, 0, keepdims=False)
    row_part = lax.dynamic_slice_in_dim(whole_pattern, sub_index * own_blocks, own_blocks, 0)
    row_part = lax.dynamic_slice_in_dim(row_part, 2 * col_blocks * front_index, 2 * col_blocks, 1)
    col_part = lax.dynamic_slice_in_dim(
        whole_pattern, 2 * col_blocks * front_index, 2 * col_blocks, 0
    )
    col_part = lax.dynamic_slice_in_dim(col_part, sub_index * own_blocks, own_blocks, 1)
    row_ids = sub_index * own_blocks + jnp.arange(own_blocks, dtype=jnp.int32)
    keep_blocks = (row_part == 1) | (col_part.T == 1) | (row_ids[:, None] == target_cols[None, :])
    keep_mask = (
        jnp.broadcast_to(keep_blocks[:, None, :, None], (own_blocks, BLK, 2 * col_blocks, BLK))
        .reshape(own_blocks * BLK, tile_cols)
        .astype(jnp.float32)
    )
    return (initial * keep_mask + merged, row_ids, target_cols)


def factor_panels(
    front_tile, row_ids, target_cols, level_depth, leaf_index, front_index, col_blocks
):
    tile_rows = front_tile.shape[0]
    panel_width = col_blocks * BLK
    row_odd = jnp.repeat(row_ids % 2 == 1, BLK)
    row_sep = jnp.repeat(row_ids // 2, BLK)
    col_odd = jnp.repeat(target_cols % 2 == 1, BLK)
    col_sep = jnp.repeat(target_cols // 2, BLK)
    factor_tile = jnp.zeros((tile_rows, col_blocks, BLK), jnp.float32)
    for step_index in range(lax.axis_size("front")):
        first_block = step_index * col_blocks
        panel_slots = first_block + jnp.arange(col_blocks, dtype=jnp.int32)
        sep_cols = front_tile.reshape(tile_rows, 2 * col_blocks, BLK)[:, 0::2].reshape(
            tile_rows, panel_width
        )
        panel_rows = spread(sep_cols, "front", step_index)
        wanted = jnp.concatenate([2 * panel_slots, target_cols])
        fetched = fetch_rows(panel_rows, wanted, level_depth, leaf_index)
        chol_block = jnp.linalg.cholesky(fetched[:panel_width])
        own_factor = solve_rows(chol_block, panel_rows)
        col_factor = solve_rows(chol_block, fetched[panel_width:])
        own_keep = (row_odd | (row_sep >= first_block + col_blocks)).astype(jnp.float32)
        col_keep = (col_odd | (col_sep >= first_block + col_blocks)).astype(jnp.float32)
        front_tile = front_tile - jnp.dot(
            own_factor * own_keep[:, None], (col_factor * col_keep[:, None]).T, precision=HIGHEST
        )
        valid_rows = (row_odd[:, None] | (row_sep[:, None] >= panel_slots[None, :])).astype(
            jnp.float32
        )
        factor_tile = jnp.where(
            front_index == step_index,
            own_factor.reshape(tile_rows, col_blocks, BLK) * valid_rows[:, :, None],
            factor_tile,
        )
    schur_tile = front_tile.reshape(tile_rows // BLK, BLK, 2 * col_blocks, BLK)[
        1::2, :, 1::2, :
    ].reshape(tile_rows // 2, col_blocks * BLK)
    return (factor_tile.reshape(tile_rows, col_blocks * BLK), schur_tile)


def per_device(
    child_updates,
    initial_one,
    initial_two,
    pattern_one,
    pattern_two,
    parent_map_one,
    parent_map_two,
):
    leaf_index = lax.axis_index("leaf")
    front_index = lax.axis_index("front")
    col_blocks = SEP // BLK // lax.axis_size("front")
    child_tile = child_updates
    factors = []
    for level_depth, initial, pattern, parent_map in (
        (1, initial_one, pattern_one, parent_map_one),
        (2, initial_two, pattern_two, parent_map_two),
    ):
        front_tile, row_ids, target_cols = assemble(
            child_tile,
            initial,
            pattern,
            parent_map,
            level_depth,
            leaf_index,
            front_index,
            col_blocks,
        )
        factor_tile, child_tile = factor_panels(
            front_tile, row_ids, target_cols, level_depth, leaf_index, front_index, col_blocks
        )
        factors.append(factor_tile)
    return (factors[0], factors[1], child_tile)


def solution(mesh):
    placed = (P("leaf", "front"), P("leaf", "front"), P("leaf", "front"), P(), P(), P(), P())
    return jax.shard_map(
        per_device,
        mesh=mesh,
        in_specs=placed,
        out_specs=(P("leaf", "front"), P("leaf", "front"), P("leaf", "front")),
        check_vma=False,
    )
```

profile of v0, /device:TPU:1, one launch (start us, length us, event | category | flops | bytes accessed | tf_op | source)
XLA Modules:
  0.0 1970.0 jit_solution(7487446941033398264)
XLA Ops:
  8.1 65.2 %all-gather.3.cloned.1.call-done = f32[1024,1024]{1,0:T(8,128)} async-done(((f32[1024,128]{1,0:T(8,128)}), f32[1024,1024]{1,0:T(8,128)}) %all-gather.3.cloned.1.call-update) | async-done | bytes 4194320 | tf_op jit(solution)/shard_map/all_gather | solution.py:72
  96.0 64.8 %all-reduce.17.cloned.1.call-done = f32[1024,128]{0,1:T(8,128)} async-done(((f32[1024,128]{0,1:T(8,128)}), f32[1024,128]{0,1:T(8,128)}) %all-reduce.17.cloned.1.call-update) | async-done | bytes 524304 | tf_op jit(solution)/shard_map/psum | solution.py:25
  198.7 67.0 %all-reduce.19.cloned.1.call-done = f32[1024,128]{0,1:T(8,128)} async-done(((f32[1024,128]{0,1:T(8,128)}), f32[1024,128]{0,1:T(8,128)}) %all-reduce.19.cloned.1.call-update) | async-done | bytes 524304 | tf_op jit(solution)/shard_map/psum | solution.py:25
  303.9 67.0 %all-reduce.21.cloned.1.call-done = f32[1024,128]{0,1:T(8,128)} async-done(((f32[1024,128]{0,1:T(8,128)}), f32[1024,128]{0,1:T(8,128)}) %all-reduce.21.cloned.1.call-update) | async-done | bytes 524304 | tf_op jit(solution)/shard_map/psum | solution.py:25
  408.9 67.0 %all-reduce.23.cloned.1.call-done = f32[1024,128]{0,1:T(8,128)} async-done(((f32[1024,128]{0,1:T(8,128)}), f32[1024,128]{0,1:T(8,128)}) %all-reduce.23.cloned.1.call-update) | async-done | bytes 524304 | tf_op jit(solution)/shard_map/psum | solution.py:25
  513.9 67.0 %all-reduce.25.cloned.1.call-done = f32[1024,128]{0,1:T(8,128)} async-done(((f32[1024,128]{0,1:T(8,128)}), f32[1024,128]{0,1:T(8,128)}) %all-reduce.25.cloned.1.call-update) | async-done | bytes 524304 | tf_op jit(solution)/shard_map/psum | solution.py:25
  619.1 67.0 %all-reduce.27.cloned.1.call-done = f32[1024,128]{0,1:T(8,128)} async-done(((f32[1024,128]{0,1:T(8,128)}), f32[1024,128]{0,1:T(8,128)}) %all-reduce.27.cloned.1.call-update) | async-done | bytes 524304 | tf_op jit(solution)/shard_map/psum | solution.py:25
  724.3 67.1 %all-reduce.29.cloned.1.call-done = f32[1024,128]{0,1:T(8,128)} async-done(((f32[1024,128]{0,1:T(8,128)}), f32[1024,128]{0,1:T(8,128)}) %all-reduce.29.cloned.1.call-update) | async-done | bytes 524304 | tf_op jit(solution)/shard_map/psum | solution.py:25
  829.3 67.1 %all-reduce.31.cloned.1.call-done = f32[1024,128]{0,1:T(8,128)} async-done(((f32[1024,128]{0,1:T(8,128)}), f32[1024,128]{0,1:T(8,128)}) %all-reduce.31.cloned.1.call-update) | async-done | bytes 524304 | tf_op jit(solution)/shard_map/psum | solution.py:25
  936.3 40.7 %all-gather.5.cloned.1.call-done = f32[512,1024]{1,0:T(8,128)} async-done(((f32[512,128]{1,0:T(8,128)}), f32[512,1024]{1,0:T(8,128)}) %all-gather.5.cloned.1.call-update) | async-done | bytes 2097168 | tf_op jit(solution)/shard_map/all_gather | solution.py:72
  987.9 15.9 collective-permute-done.9
  1016.5 65.7 %all-reduce.33.cloned.1.call-done = f32[512,128]{0,1:T(8,128)} async-done(((f32[512,128]{0,1:T(8,128)}), f32[512,128]{0,1:T(8,128)}) %all-reduce.33.cloned.1.call-update) | async-done | bytes 262160 | tf_op jit(solution)/shard_map/psum | solution.py:25
  1091.7 11.8 collective-permute-done.12
  1132.3 67.0 %all-reduce.35.cloned.1.call-done = f32[512,128]{0,1:T(8,128)} async-done(((f32[512,128]{0,1:T(8,128)}), f32[512,128]{0,1:T(8,128)}) %all-reduce.35.cloned.1.call-update) | async-done | bytes 262160 | tf_op jit(solution)/shard_map/psum | solution.py:25
  1208.6 11.8 collective-permute-done.14
  1249.3 67.1 %all-reduce.37.cloned.1.call-done = f32[512,128]{0,1:T(8,128)} async-done(((f32[512,128]{0,1:T(8,128)}), f32[512,128]{0,1:T(8,128)}) %all-reduce.37.cloned.1.call-update) | async-done | bytes 262160 | tf_op jit(solution)/shard_map/psum | solution.py:25
  1366.4 67.0 %all-reduce.39.cloned.1.call-done = f32[512,128]{0,1:T(8,128)} async-done(((f32[512,128]{0,1:T(8,128)}), f32[512,128]{0,1:T(8,128)}) %all-reduce.39.cloned.1.call-update) | async-done | bytes 262160 | tf_op jit(solution)/shard_map/psum | solution.py:25
  1442.7 11.8 collective-permute-done.18
  1483.5 67.0 %all-reduce.41.cloned.1.call-done = f32[512,128]{0,1:T(8,128)} async-done(((f32[512,128]{0,1:T(8,128)}), f32[512,128]{0,1:T(8,128)}) %all-reduce.41.cloned.1.call-update) | async-done | bytes 262160 | tf_op jit(solution)/shard_map/psum | solution.py:25
  1560.0 11.8 collective-permute-done.20
  1600.8 67.0 %all-reduce.43.cloned.1.call-done = f32[512,128]{0,1:T(8,128)} async-done(((f32[512,128]{0,1:T(8,128)}), f32[512,128]{0,1:T(8,128)}) %all-reduce.43.cloned.1.call-update) | async-done | bytes 262160 | tf_op jit(solution)/shard_map/psum | solution.py:25
  1677.0 11.8 collective-permute-done.22
  1718.5 67.0 %all-reduce.45.cloned.1.call-done = f32[512,128]{0,1:T(8,128)} async-done(((f32[512,128]{0,1:T(8,128)}), f32[512,128]{0,1:T(8,128)}) %all-reduce.45.cloned.1.call-update) | async-done | bytes 262160 | tf_op jit(solution)/shard_map/psum | solution.py:25
  1840.7 67.0 %all-reduce.47.cloned.1.call-done = f32[512,128]{0,1:T(8,128)} async-done(((f32[512,128]{0,1:T(8,128)}), f32[512,128]{0,1:T(8,128)}) %all-reduce.47.cloned.1.call-update) | async-done | bytes 262160 | tf_op jit(solution)/shard_map/psum | solution.py:25
  (641 shorter events, 702.4 us)
Async XLA Ops:
  7.2 66.1 %all-gather.3.cloned.1.call-start = ((), (), s32[]{:S(2)}) async-start(), calls=%async_computation | async-start | bytes 4718592 | tf_op jit(solution)/shard_map/all_gather | solution.py:72
  7.9 152.8 %all-reduce.17.cloned.1.call-start = ((), (), s32[]{:S(2)}) async-start(), calls=%async_computation.1 | async-start | bytes 1048576 | tf_op jit(solution)/shard_map/psum | solution.py:25
  95.8 169.9 %all-reduce.19.cloned.1.call-start = ((), (), s32[]{:S(2)}) async-start(), calls=%async_computation.2 | async-start | bytes 1048576 | tf_op jit(solution)/shard_map/psum | solution.py:25
  198.6 172.3 %all-reduce.21.cloned.1.call-start = ((), (), s32[]{:S(2)}) async-start(), calls=%async_computation.3 | async-start | bytes 1048576 | tf_op jit(solution)/shard_map/psum | solution.py:25
  303.8 172.1 %all-reduce.23.cloned.1.call-start = ((), (), s32[]{:S(2)}) async-start(), calls=%async_computation.4 | async-start | bytes 1048576 | tf_op jit(solution)/shard_map/psum | solution.py:25
  408.7 172.2 %all-reduce.25.cloned.1.call-start = ((), (), s32[]{:S(2)}) async-start(), calls=%async_computation.5 | async-start | bytes 1048576 | tf_op jit(solution)/shard_map/psum | solution.py:25
  513.9 172.2 %all-reduce.27.cloned.1.call-start = ((), (), s32[]{:S(2)}) async-start(), calls=%async_computation.6 | async-start | bytes 1048576 | tf_op jit(solution)/shard_map/psum | solution.py:25
  619.0 172.4 %all-reduce.29.cloned.1.call-start = ((), (), s32[]{:S(2)}) async-start(), calls=%async_computation.7 | async-start | bytes 1048576 | tf_op jit(solution)/shard_map/psum | solution.py:25
  724.2 172.1 %all-reduce.31.cloned.1.call-start = ((), (), s32[]{:S(2)}) async-start(), calls=%async_computation.8 | async-start | bytes 1048576 | tf_op jit(solution)/shard_map/psum | solution.py:25
  829.2 147.8 %all-gather.5.cloned.1.call-start = ((), (), s32[]{:S(2)}) async-start(), calls=%async_computation.9 | async-start | bytes 2359296 | tf_op jit(solution)/shard_map/all_gather | solution.py:72
  935.2 147.0 %all-reduce.33.cloned.1.call-start = ((), (), s32[]{:S(2)}) async-start(), calls=%async_computation.10 | async-start | bytes 524288 | tf_op jit(solution)/shard_map/psum | solution.py:25
  983.8 20.0 %collective-permute-start.9 = (f32[1024,256]{0,1:T(8,128)}, f32[1024,256]{0,1:T(8,128)}, u32[]{:S(2)}, u32[]{:S(2)}) collective-permute-start(f32[1024,256]{0,1:T(8,128)} %copy.86), channel_id=1, source_target_pairs={{0,16},{16,0},{8,24},{24,8},{32,48},{48,32},{40,56},{56,40},{64,80... | collective-permute-start | bytes 3145736 | tf_op jit(solution)/shard_map/ppermute | solution.py:20
  1016.5 182.9 %all-reduce.35.cloned.1.call-start = ((), (), s32[]{:S(2)}) async-start(), calls=%async_computation.11 | async-start | bytes 524288 | tf_op jit(solution)/shard_map/psum | solution.py:25
  1089.8 13.7 collective-permute-start.12
  1132.3 184.1 %all-reduce.37.cloned.1.call-start = ((), (), s32[]{:S(2)}) async-start(), calls=%async_computation.12 | async-start | bytes 524288 | tf_op jit(solution)/shard_map/psum | solution.py:25
  1249.3 184.1 %all-reduce.39.cloned.1.call-start = ((), (), s32[]{:S(2)}) async-start(), calls=%async_computation.13 | async-start | bytes 524288 | tf_op jit(solution)/shard_map/psum | solution.py:25
  1366.4 184.1 %all-reduce.41.cloned.1.call-start = ((), (), s32[]{:S(2)}) async-start(), calls=%async_computation.14 | async-start | bytes 524288 | tf_op jit(solution)/shard_map/psum | solution.py:25
  1441.1 13.5 collective-permute-start.18
  1483.4 184.4 %all-reduce.43.cloned.1.call-start = ((), (), s32[]{:S(2)}) async-start(), calls=%async_computation.15 | async-start | bytes 524288 | tf_op jit(solution)/shard_map/psum | solution.py:25
  1558.2 13.7 collective-permute-start.20
  1600.7 184.8 %all-reduce.45.cloned.1.call-start = ((), (), s32[]{:S(2)}) async-start(), calls=%async_computation.16 | async-start | bytes 524288 | tf_op jit(solution)/shard_map/psum | solution.py:25
  1718.4 189.3 %all-reduce.47.cloned.1.call-start = ((), (), s32[]{:S(2)}) async-start(), calls=%async_computation.17 | async-start | bytes 524288 | tf_op jit(solution)/shard_map/psum | solution.py:25
  1793.2 13.4 collective-permute-start.24
  1916.1 13.7 collective-permute-start.26
  (89 other events, 3465.6 us)
Sparse Core Ops, SparseCore 0:
  9.7 63.4 all-gather.2
  95.9 64.7 all-reduce.16
  198.7 66.9 all-reduce.18
  303.9 66.9 all-reduce.20
  408.9 67.0 all-reduce.22
  514.0 66.9 all-reduce.24
  619.1 66.9 all-reduce.26
  724.3 66.9 all-reduce.28
  829.3 66.9 all-reduce.30
  935.3 41.6 all-gather.4
  1016.6 65.5 all-reduce.32
  1132.4 66.9 all-reduce.34
  1249.4 66.9 all-reduce.36
  1366.5 66.9 all-reduce.38
  1483.5 66.9 all-reduce.40
  1600.8 66.9 all-reduce.42
  1718.6 66.9 all-reduce.44
  1840.7 66.9 all-reduce.46
where the time goes:
time: 1980 us; the launch traced here: 1970 us
  waiting for transfers between devices  1300 us (66%)
  other arithmetic  415 us (21%)
  starting transfers between devices  111 us (6%)
  local copies, waits for them, and re-layouts  86 us (4%)
  matrix products  35.7 us (2%)
    psum x16, waiting for transfers between devices, spread(): return lax.psum(block, axis)  1070 us
    another operation x48, other arithmetic, factor_panels(): chol_block = jnp.linalg.cholesky(fetched[:panel_width])  198 us
    another operation x32, other arithmetic, solve_rows(): jax.scipy.linalg.solve_triangular(chol_block, right_side.T, lower=True)  168 us
    ppermute x27, waiting for transfers between devices, swapped(): return lax.ppermute(block, axis, route)  128 us
    ppermute x27, starting transfers between devices, swapped(): return lax.ppermute(block, axis, route)  110 us
    all_gather x2, waiting for transfers between devices, assemble(): gathered = lax.all_gather(child_tile, 'front', axis=1, tiled=True)  106 us
  transfers between devices with their start and end apart: 45, of which 43 were waited for; matrix products, arithmetic and copies ran while one was open for 1% of the time, Pallas kernels for 0%

commit v1 on v0

--- a/solution.py
+++ b/solution.py
@@ -22,7 +22,7 @@
 
 def spread(block, axis, holder):
     block = jnp.where(lax.axis_index(axis) == holder, block, jnp.zeros_like(block))
-    return lax.psum(block, axis)
+    return jnp.sum(jax.lax.all_gather(block, axis_name=axis), 0)
 
 
 def solve_rows(chol_block, right_side):

time: 1980 us -> 1650 us (0.83)
  waiting for transfers between devices: 1300 us -> 946 us
  local copies, waits for them, and re-layouts: 86 us -> 164 us
  starting transfers between devices: 111 us -> 72.4 us
    psum x16 -> x0, waiting for transfers between devices: 1070 us -> none  [spread(): return lax.psum(block, axis)]
    all_gather x0 -> x16, waiting for transfers between devices: none -> 713 us  [spread(): return jnp.sum(jax.lax.all_gather(block, axis_name=axis), 0)]
    unnamed x143 -> x113, local copies, waits for them, and re-layouts: 12.7 us -> 81.6 us
    ppermute x27, starting transfers between devices: 110 us -> 69.4 us  [swapped(): return lax.ppermute(block, axis, route)]
where the time goes in v1:
time: 1650 us
  waiting for transfers between devices  946 us (57%)
  other arithmetic  413 us (25%)
  local copies, waits for them, and re-layouts  164 us (10%)
  starting transfers between devices  72.4 us (4%)
  matrix products  33.4 us (2%)
  between operations  17.5 us (1%)
    all_gather x16, waiting for transfers between devices, spread(): return jnp.sum(jax.lax.all_gather(block, axis_name=axis), 0)  713 us
    another operation x48, other arithmetic, factor_panels(): chol_block = jnp.linalg.cholesky(fetched[:panel_width])  198 us
    another operation x32, other arithmetic, solve_rows(): jax.scipy.linalg.solve_triangular(chol_block, right_side.T, lower=True)  167 us
    ppermute x27, waiting for transfers between devices, swapped(): return lax.ppermute(block, axis, route)  127 us
    all_gather x2, waiting for transfers between devices, assemble(): gathered = lax.all_gather(child_tile, 'front', axis=1, tiled=True)  106 us
    unnamed x113, local copies, waits for them, and re-layouts  81.6 us
    ppermute x27, starting transfers between devices, swapped(): return lax.ppermute(block, axis, route)  69.4 us
  transfers between devices with their start and end apart: 45, of which 43 were waited for; matrix products, arithmetic and copies ran while one was open for 1% of the time, Pallas kernels for 0%

profile of v1, /device:TPU:1, one launch (start us, length us, event | category | flops | bytes accessed | tf_op | source)
XLA Modules:
  0.0 1646.5 jit_solution(13409655176662429897)
XLA Ops:
  8.1 65.2 %all-gather.35.cloned.1.call-done = f32[1024,1024]{1,0:T(8,128)} async-done(((f32[1024,128]{1,0:T(8,128)}), f32[1024,1024]{1,0:T(8,128)}) %all-gather.35.cloned.1.call-update) | async-done | bytes 4194320 | tf_op jit(solution)/shard_map/all_gather | solution.py:72
  96.3 50.5 %all-gather.39.cloned.1.call-done = f32[8192,1,128]{0,2,1:T(8,128)} async-done(((f32[1024,1,128]{0,2,1:T(8,128)}), f32[8192,1,128]{0,2,1:T(8,128)}) %all-gather.39.cloned.1.call-update) | async-done | bytes 4194320 | tf_op jit(solution)/shard_map/all_gather | solution.py:25
  185.7 53.0 %all-gather.41.cloned.1.call-done = f32[8192,1,128]{0,2,1:T(8,128)} async-done(((f32[1024,1,128]{0,2,1:T(8,128)}), f32[8192,1,128]{0,2,1:T(8,128)}) %all-gather.41.cloned.1.call-update) | async-done | bytes 4194320 | tf_op jit(solution)/shard_map/all_gather | solution.py:25
  277.6 52.9 %all-gather.43.cloned.1.call-done = f32[8192,1,128]{0,2,1:T(8,128)} async-done(((f32[1024,1,128]{0,2,1:T(8,128)}), f32[8192,1,128]{0,2,1:T(8,128)}) %all-gather.43.cloned.1.call-update) | async-done | bytes 4194320 | tf_op jit(solution)/shard_map/all_gather | solution.py:25
  369.8 52.6 %all-gather.45.cloned.1.call-done = f32[8192,1,128]{0,2,1:T(8,128)} async-done(((f32[1024,1,128]{0,2,1:T(8,128)}), f32[8192,1,128]{0,2,1:T(8,128)}) %all-gather.45.cloned.1.call-update) | async-done | bytes 4194320 | tf_op jit(solution)/shard_map/all_gather | solution.py:25
  463.3 53.0 %all-gather.47.cloned.1.call-done = f32[8192,1,128]{0,2,1:T(8,128)} async-done(((f32[1024,1,128]{0,2,1:T(8,128)}), f32[8192,1,128]{0,2,1:T(8,128)}) %all-gather.47.cloned.1.call-update) | async-done | bytes 4194320 | tf_op jit(solution)/shard_map/all_gather | solution.py:25
  557.4 52.9 %all-gather.49.cloned.1.call-done = f32[8192,1,128]{0,2,1:T(8,128)} async-done(((f32[1024,1,128]{0,2,1:T(8,128)}), f32[8192,1,128]{0,2,1:T(8,128)}) %all-gather.49.cloned.1.call-update) | async-done | bytes 4194320 | tf_op jit(solution)/shard_map/all_gather | solution.py:25
  651.6 53.1 %all-gather.51.cloned.1.call-done = f32[8192,1,128]{0,2,1:T(8,128)} async-done(((f32[1024,1,128]{0,2,1:T(8,128)}), f32[8192,1,128]{0,2,1:T(8,128)}) %all-gather.51.cloned.1.call-update) | async-done | bytes 4194320 | tf_op jit(solution)/shard_map/all_gather | solution.py:25
  745.7 53.0 %all-gather.53.cloned.1.call-done = f32[8192,1,128]{0,2,1:T(8,128)} async-done(((f32[1024,1,128]{0,2,1:T(8,128)}), f32[8192,1,128]{0,2,1:T(8,128)}) %all-gather.53.cloned.1.call-update) | async-done | bytes 4194320 | tf_op jit(solution)/shard_map/all_gather | solution.py:25
  841.5 40.9 %all-gather.37.cloned.1.call-done = f32[512,1024]{1,0:T(8,128)} async-done(((f32[512,128]{1,0:T(8,128)}), f32[512,1024]{1,0:T(8,128)}) %all-gather.37.cloned.1.call-update) | async-done | bytes 2097168 | tf_op jit(solution)/shard_map/all_gather | solution.py:72
  896.6 14.9 collective-permute-done.9
  925.2 35.1 %all-gather.55.cloned.1.call-done = f32[4096,1,128]{0,2,1:T(8,128)} async-done(((f32[512,1,128]{0,2,1:T(8,128)}), f32[4096,1,128]{0,2,1:T(8,128)}) %all-gather.55.cloned.1.call-update) | async-done | bytes 2097168 | tf_op jit(solution)/shard_map/all_gather | solution.py:25
  971.4 11.8 collective-permute-done.12
  1012.1 36.6 %all-gather.57.cloned.1.call-done = f32[4096,1,128]{0,2,1:T(8,128)} async-done(((f32[512,1,128]{0,2,1:T(8,128)}), f32[4096,1,128]{0,2,1:T(8,128)}) %all-gather.57.cloned.1.call-update) | async-done | bytes 2097168 | tf_op jit(solution)/shard_map/all_gather | solution.py:25
  1059.9 11.8 collective-permute-done.14
  1101.5 36.6 %all-gather.59.cloned.1.call-done = f32[4096,1,128]{0,2,1:T(8,128)} async-done(((f32[512,1,128]{0,2,1:T(8,128)}), f32[4096,1,128]{0,2,1:T(8,128)}) %all-gather.59.cloned.1.call-update) | async-done | bytes 2097168 | tf_op jit(solution)/shard_map/all_gather | solution.py:25
  1149.1 11.8 collective-permute-done.16
  1189.9 36.6 %all-gather.61.cloned.1.call-done = f32[4096,1,128]{0,2,1:T(8,128)} async-done(((f32[512,1,128]{0,2,1:T(8,128)}), f32[4096,1,128]{0,2,1:T(8,128)}) %all-gather.61.cloned.1.call-update) | async-done | bytes 2097168 | tf_op jit(solution)/shard_map/all_gather | solution.py:25
  1279.1 36.6 %all-gather.63.cloned.1.call-done = f32[4096,1,128]{0,2,1:T(8,128)} async-done(((f32[512,1,128]{0,2,1:T(8,128)}), f32[4096,1,128]{0,2,1:T(8,128)}) %all-gather.63.cloned.1.call-update) | async-done | bytes 2097168 | tf_op jit(solution)/shard_map/all_gather | solution.py:25
  1326.8 11.9 collective-permute-done.20
  1367.7 36.6 %all-gather.65.cloned.1.call-done = f32[4096,1,128]{0,2,1:T(8,128)} async-done(((f32[512,1,128]{0,2,1:T(8,128)}), f32[4096,1,128]{0,2,1:T(8,128)}) %all-gather.65.cloned.1.call-update) | async-done | bytes 2097168 | tf_op jit(solution)/shard_map/all_gather | solution.py:25
  1456.8 36.6 %all-gather.67.cloned.1.call-done = f32[4096,1,128]{0,2,1:T(8,128)} async-done(((f32[512,1,128]{0,2,1:T(8,128)}), f32[4096,1,128]{0,2,1:T(8,128)}) %all-gather.67.cloned.1.call-update) | async-done | bytes 2097168 | tf_op jit(solution)/shard_map/all_gather | solution.py:25
  1504.5 11.8 collective-permute-done.24
  1545.2 36.7 %all-gather.69.cloned.1.call-done = f32[4096,1,128]{0,2,1:T(8,128)} async-done(((f32[512,1,128]{0,2,1:T(8,128)}), f32[4096,1,128]{0,2,1:T(8,128)}) %all-gather.69.cloned.1.call-update) | async-done | bytes 2097168 | tf_op jit(solution)/shard_map/all_gather | solution.py:25
  (619 shorter events, 736.0 us)
Async XLA Ops:
  7.2 66.1 %all-gather.35.cloned.1.call-start = ((), (), s32[]{:S(2)}) async-start(), calls=%async_computation | async-start | bytes 4718592 | tf_op jit(solution)/shard_map/all_gather | solution.py:72
  7.9 138.8 %all-gather.39.cloned.1.call-start = ((), (), s32[]{:S(2)}) async-start(), calls=%async_computation.2 | async-start | bytes 4718592 | tf_op jit(solution)/shard_map/all_gather | solution.py:25
  95.8 143.0 %all-gather.41.cloned.1.call-start = ((), (), s32[]{:S(2)}) async-start(), calls=%async_computation.3 | async-start | bytes 4718592 | tf_op jit(solution)/shard_map/all_gather | solution.py:25
  185.5 145.0 %all-gather.43.cloned.1.call-start = ((), (), s32[]{:S(2)}) async-start(), calls=%async_computation.4 | async-start | bytes 4718592 | tf_op jit(solution)/shard_map/all_gather | solution.py:25
  277.3 145.1 %all-gather.45.cloned.1.call-start = ((), (), s32[]{:S(2)}) async-start(), calls=%async_computation.5 | async-start | bytes 4718592 | tf_op jit(solution)/shard_map/all_gather | solution.py:25
  369.1 147.2 %all-gather.47.cloned.1.call-start = ((), (), s32[]{:S(2)}) async-start(), calls=%async_computation.6 | async-start | bytes 4718592 | tf_op jit(solution)/shard_map/all_gather | solution.py:25
  463.0 147.3 %all-gather.49.cloned.1.call-start = ((), (), s32[]{:S(2)}) async-start(), calls=%async_computation.7 | async-start | bytes 4718592 | tf_op jit(solution)/shard_map/all_gather | solution.py:25
  557.1 147.6 %all-gather.51.cloned.1.call-start = ((), (), s32[]{:S(2)}) async-start(), calls=%async_computation.8 | async-start | bytes 4718592 | tf_op jit(solution)/shard_map/all_gather | solution.py:25
  651.4 147.3 %all-gather.53.cloned.1.call-start = ((), (), s32[]{:S(2)}) async-start(), calls=%async_computation.9 | async-start | bytes 4718592 | tf_op jit(solution)/shard_map/all_gather | solution.py:25
  745.4 137.1 %all-gather.37.cloned.1.call-start = ((), (), s32[]{:S(2)}) async-start(), calls=%async_computation.1 | async-start | bytes 2359296 | tf_op jit(solution)/shard_map/all_gather | solution.py:72
  840.5 119.9 %all-gather.55.cloned.1.call-start = ((), (), s32[]{:S(2)}) async-start(), calls=%async_computation.10 | async-start | bytes 2359296 | tf_op jit(solution)/shard_map/all_gather | solution.py:25
  891.5 20.0 %collective-permute-start.9 = (f32[1024,256]{0,1:T(8,128)}, f32[1024,256]{0,1:T(8,128)}, u32[]{:S(2)}, u32[]{:S(2)}) collective-permute-start(f32[1024,256]{0,1:T(8,128)} %copy.155), channel_id=1, source_target_pairs={{0,16},{16,0},{8,24},{24,8},{32,48},{48,32},{40,56},{56,40},{64,80... | collective-permute-start | bytes 3145736 | tf_op jit(solution)/shard_map/ppermute | solution.py:20
  925.2 123.6 %all-gather.57.cloned.1.call-start = ((), (), s32[]{:S(2)}) async-start(), calls=%async_computation.11 | async-start | bytes 2359296 | tf_op jit(solution)/shard_map/all_gather | solution.py:25
  1012.1 126.0 %all-gather.59.cloned.1.call-start = ((), (), s32[]{:S(2)}) async-start(), calls=%async_computation.12 | async-start | bytes 2359296 | tf_op jit(solution)/shard_map/all_gather | solution.py:25
  1058.2 13.6 collective-permute-start.14
  1101.4 125.0 %all-gather.61.cloned.1.call-start = ((), (), s32[]{:S(2)}) async-start(), calls=%async_computation.13 | async-start | bytes 2359296 | tf_op jit(solution)/shard_map/all_gather | solution.py:25
  1189.8 125.9 %all-gather.63.cloned.1.call-start = ((), (), s32[]{:S(2)}) async-start(), calls=%async_computation.14 | async-start | bytes 2359296 | tf_op jit(solution)/shard_map/all_gather | solution.py:25
  1235.9 13.4 collective-permute-start.18
  1279.0 125.3 %all-gather.65.cloned.1.call-start = ((), (), s32[]{:S(2)}) async-start(), calls=%async_computation.15 | async-start | bytes 2359296 | tf_op jit(solution)/shard_map/all_gather | solution.py:25
  1325.1 13.6 collective-permute-start.20
  1367.6 125.8 %all-gather.67.cloned.1.call-start = ((), (), s32[]{:S(2)}) async-start(), calls=%async_computation.16 | async-start | bytes 2359296 | tf_op jit(solution)/shard_map/all_gather | solution.py:25
  1456.8 125.1 %all-gather.69.cloned.1.call-start = ((), (), s32[]{:S(2)}) async-start(), calls=%async_computation.17 | async-start | bytes 2359296 | tf_op jit(solution)/shard_map/all_gather | solution.py:25
  1502.9 13.4 collective-permute-start.24
  1591.3 13.6 collective-permute-start.26
  (66 other events, 685.7 us)
Sparse Core Ops, SparseCore 0:
  9.7 63.5 all-gather.34
  95.9 50.7 all-gather.38
  185.6 53.1 all-gather.40
  277.4 53.1 all-gather.42
  369.2 53.1 all-gather.44
  463.1 53.1 all-gather.46
  557.2 53.1 all-gather.48
  651.5 53.1 all-gather.50
  745.5 53.1 all-gather.52
  840.6 41.8 all-gather.36
  925.3 34.9 all-gather.54
  1012.2 36.5 all-gather.56
  1101.6 36.5 all-gather.58
  1189.9 36.5 all-gather.60
  1279.1 36.5 all-gather.62
  1367.7 36.5 all-gather.64
  1456.9 36.5 all-gather.66
  1545.3 36.5 all-gather.68
